TPU v7x, 256 devices: a whole 4x4x8 slice. The times are simulated.
256 devices in a mesh: leaf: 16 (over y, z_lo), draw: 16 (over z_hi, x, core).
Axes of the slice: x: 4, y: 4, z: 8 (z_hi: 2, z_lo: 4; z = z_hi * 4 + z_lo), core: 2. Of those that a mesh axis runs over, the one named last changes fastest.
Arguments:
- noise_draws: bfloat16 [3, 32, 256, 8192], P(None, 'leaf', None, 'draw'), may hold values from -6 to 6
- inverse_diagonal: bfloat16 [3, 32, 256, 256], P(None, 'leaf', 'draw'), as said below
- coupling_blocks: bfloat16 [2, 32, 16, 256, 256], P(None, 'leaf', 'draw'), may hold values from -0.0625 to 0.0625
- ancestor_pick: int32 [2, 16, 16], replicated, may hold values from 0 to 1
- coupling_lists: int32 [2, 32, 16], P(None, 'leaf'), may hold values from 0 to 31, as said below
- live_counts: int32 [2, 32], P(None, 'leaf'), may hold values from 1 to 16, as said below
Outputs:
- samples: bfloat16 [3, 32, 256, 8192], P(None, 'leaf', None, 'draw')
Inputs may be any that keep to these rules, and one draw needn't show every extreme that they name: `coupling_lists`: the 16 entries of one supernode are distinct. Level 1 entries are below 16, and the live entries of the 2 level-1 supernodes of one owner together name every owner. In level 2 the first 8 entries are 16 or more and the rest below 16; the first halves of one owner's level-2 supernodes together name every value from 16 to 31. `live_counts`: the level-1 counts of one owner's 2 supernodes sum to more than 16; level-2 counts are 8 or more; in each level some supernode has 16. `inverse_diagonal`: each block is lower triangular, with diagonal entries between 0.6 and 1.4.
All inputs are finite; a program needn't handle non-finite values.
Results may differ from a plain program's by a relative error of at most 0.0052.
Values may be sent and summed in bfloat16 or wider, within the bound.
A program may use at most 64 MiB of HBM per device.

v0:
```python
import jax
import jax.numpy as jnp
from jax import lax
from jax.sharding import PartitionSpec as P


def inverse_fold(right_side, piece):
    return jnp.einsum("nrc,nrs->ncs", piece, right_side, preferred_element_type=jnp.float32)


def apply_inverse(inverse_part, right_side):
    solved = inverse_fold(right_side, lax.all_gather(inverse_part, "draw", axis=1, tiled=True))
    return solved.astype(jnp.bfloat16)


def coupling_fold(table, rows_used, counts_here):
    most = jnp.max(counts_here)

    def fold(carry, piece, start):
        width = piece.shape[1]
        stop = jnp.clip(most, 0, width)

        def turn(offset, total):
            wanted = lax.dynamic_index_in_dim(rows_used, offset, 1, keepdims=False)
            picked = jnp.take(table, wanted, axis=0)
            alive = (offset < counts_here).astype(jnp.bfloat16)
            picked = picked * alive[:, None, None]
            block = lax.dynamic_index_in_dim(piece, offset, 1, keepdims=False)
            return total + jnp.einsum(
                "nrc,nrs->ncs", block, picked, preferred_element_type=jnp.float32
            )

        return lax.fori_loop(0, stop, turn, carry)

    return fold


def gather_updates(block_part, table, rows_used, counts_here, shape):
    empty = jnp.zeros(shape, jnp.float32)
    fold = coupling_fold(table, rows_used, counts_here)
    return fold(empty, lax.all_gather(block_part, "draw", axis=1, tiled=True), jnp.int32(0))


def share_level(solved, picks_level, myself):
    chosen = lax.dynamic_index_in_dim(picks_level, myself, 1, keepdims=False)
    outgoing = jnp.take(solved, chosen, axis=0)
    return lax.all_to_all(outgoing, "leaf", split_axis=0, concat_axis=0, tiled=True)


def on_device(
    noise_draws, inverse_diagonal, coupling_blocks, ancestor_pick, coupling_lists, live_counts
):
    myself = lax.axis_index("leaf")
    inverse_all, blocks_all = (inverse_diagonal, coupling_blocks)
    solved = apply_inverse(inverse_all[0], noise_draws[0])
    levels_done = [solved]
    tables = []
    for level in range(1, noise_draws.shape[0]):
        tables.append(share_level(levels_done[-1], ancestor_pick[level - 1], myself))
        table = jnp.concatenate(tables, axis=0)
        rows_used = coupling_lists[level - 1]
        updates = gather_updates(
            blocks_all[level - 1], table, rows_used, live_counts[level - 1], solved.shape
        )
        right_side = (noise_draws[level].astype(jnp.float32) - updates).astype(jnp.bfloat16)
        levels_done.append(apply_inverse(inverse_all[level], right_side))
    return jnp.stack(levels_done, axis=0)


def solution(mesh):
    placed = (
        P(None, "leaf", None, "draw"),
        P(None, "leaf", "draw", None),
        P(None, "leaf", "draw", None, None),
        P(),
        P(None, "leaf", None),
        P(None, "leaf"),
    )
    return jax.shard_map(
        on_device,
        mesh=mesh,
        in_specs=placed,
        out_specs=P(None, "leaf", None, "draw"),
        check_vma=False,
    )
```

profile of v0, /device:TPU:24, one launch (start us, length us, event | category | flops | bytes accessed | tf_op | source)
XLA Modules:
  0.0 495.0 jit_solution(10625036051095000772)
XLA Ops:
  8.2 33.8 %all-gather = bf16[1,2,256,256]{3,1,0,2:T(2,128)(2,1)S(1)} all-gather(bf16[1,2,16,256]{3,1,0,2:T(2,128)(2,1)S(1)} %copy.43), channel_id=2, replica_groups=mesh['leaf'=16,'draw'=16] {'draw'}, dimensions={2}, use_global_device_ids=true | all-gather | bytes 278528 | tf_op jit(solution)/shard_map/all_gather | solution.py:12
  43.6 2.8 gather_fusion.2
  46.4 4.6 broadcast_select_fusion.1
  51.0 6.2 %all-to-all-start = ((bf16[16,256,512]{2,1,0:T(8,128)(2,1)}), bf16[16,256,512]{2,1,0:T(8,128)(2,1)}, u32[]{:S(2)}, u32[]{:S(2)}) async-start(bf16[16,256,512]{2,1,0:T(8,128)(2,1)} %broadcast_select_fusion.1), calls=%async_computation | async-start | bytes 8388608 | tf_op jit(solution)/shard_map/all_to_all | solution.py:47
  59.6 99.0 %all-gather.2 = bf16[1,2,256,256]{3,2,1,0:T(8,128)(2,1)S(1)} all-gather(bf16[1,2,16,256]{3,2,1,0:T(8,128)(2,1)S(1)} %get-tuple-element.164), channel_id=4, replica_groups=mesh['leaf'=16,'draw'=16] {'draw'}, dimensions={2}, use_global_device_ids=true | all-gather | bytes 278528 | tf_op jit(solution)/shard_map/all_gather | solution.py:12
  158.7 23.4 %all-to-all-done = bf16[16,256,512]{2,1,0:T(8,128)(2,1)} async-done(((bf16[16,256,512]{2,1,0:T(8,128)(2,1)}), bf16[16,256,512]{2,1,0:T(8,128)(2,1)}, u32[]{:S(2)}, u32[]{:S(2)}) %all-to-all-start) | async-done | bytes 4194336 | tf_op jit(solution)/shard_map/all_to_all | solution.py:47
  182.2 60.5 %while.20 = (s32[]{:T(128)}, f32[2,256,512]{2,1,0:T(8,128)S(1)}, s32[]{:T(128)}, bf16[2,16,256,256]{3,2,0,1:T(8,128)(2,1)}, s32[2,16]{0,1:T(8,128)S(1)}, /*index...) while((s32[]{:T(128)}, f32[2,256,512]{2,1,0:T(8,128)S(1)}, s32[]{:T(128)}, ...), condition=%wide.region_2.4_spmd, body=%wide.region_1.3_spmd.sunk | while | flops 135005200 | bytes 3936455 | solution.py:33
  182.2 2.8 gather_fusion
  190.9 2.8 gather_fusion
  195.2 2.8 gather_fusion
  246.8 4.6 broadcast_select_fusion
  251.4 14.8 %all-to-all-start.1 = ((bf16[16,256,512]{2,1,0:T(8,128)(2,1)}), bf16[16,256,512]{2,1,0:T(8,128)(2,1)}, u32[]{:S(2)}, u32[]{:S(2)}) async-start(bf16[16,256,512]{2,1,0:T(8,128)(2,1)} %broadcast_select_fusion), calls=%async_computation.1 | async-start | bytes 8388608 | tf_op jit(solution)/shard_map/all_to_all | solution.py:47
  267.7 96.3 %all-gather.4 = bf16[1,2,256,256]{3,2,1,0:T(8,128)(2,1)S(1)} all-gather(bf16[1,2,16,256]{3,2,1,0:T(8,128)(2,1)S(1)} %get-tuple-element.162), channel_id=6, replica_groups=mesh['leaf'=16,'draw'=16] {'draw'}, dimensions={2}, use_global_device_ids=true | all-gather | bytes 278528 | tf_op jit(solution)/shard_map/all_gather | solution.py:12
  364.0 25.7 %all-to-all-done.1 = bf16[16,256,512]{2,1,0:T(8,128)(2,1)} async-done(((bf16[16,256,512]{2,1,0:T(8,128)(2,1)}), bf16[16,256,512]{2,1,0:T(8,128)(2,1)}, u32[]{:S(2)}, u32[]{:S(2)}) %all-to-all-start.1) | async-done | bytes 4194336 | tf_op jit(solution)/shard_map/all_to_all | solution.py:47
  389.6 7.4 %pad_maximum_fusion = bf16[32,256,512]{2,1,0:T(8,128)(2,1)} fusion(bf16[16,256,512]{2,1,0:T(8,128)(2,1)} %all-to-all-done.1, bf16[16,256,512]{2,1,0:T(8,128)(2,1)} %all-to-all-done), kind=kLoop, calls=%fused_computation.32 | loop fusion | flops 4194304 | bytes 16777216 | tf_op jit(solution)/shard_map/concatenate | solution.py:60
  397.2 88.3 %while.21 = (s32[]{:T(128)}, f32[2,256,512]{2,1,0:T(8,128)S(1)}, s32[]{:T(128)}, bf16[2,16,256,256]{3,2,0,1:T(8,128)(2,1)}, s32[2,16]{0,1:T(8,128)S(1)}, /*index...) while((s32[]{:T(128)}, f32[2,256,512]{2,1,0:T(8,128)S(1)}, s32[]{:T(128)}, ...), condition=%wide.region_5.7_spmd, body=%wide.region_4.6_spmd.sunk | while | flops 135005200 | bytes 3936455 | solution.py:33
  397.2 4.0 gather_fusion.1
  402.8 4.0 gather_fusion.1
  408.3 4.0 gather_fusion.1
  413.8 4.0 gather_fusion.1
  419.3 4.0 gather_fusion.1
  424.8 4.0 gather_fusion.1
  430.3 4.0 gather_fusion.1
  435.8 4.0 gather_fusion.1
  441.4 4.0 gather_fusion.1
  446.9 4.0 gather_fusion.1
  452.4 4.0 gather_fusion.1
  457.9 4.0 gather_fusion.1
  463.4 4.0 gather_fusion.1
  468.9 4.0 gather_fusion.1
  474.5 4.0 gather_fusion.1
  480.0 4.0 gather_fusion.1
  (167 shorter events, 88.2 us)
Async XLA Ops:
  51.0 6.3 %copy-start = (bf16[2,2,1,256,256]{4,3,2,1,0:T(8,128)(2,1)S(1)}, bf16[2,2,1,256,256]{4,3,2,1,0:T(8,128)(2,1)}, u32[]{:S(2)}) copy-start(bf16[2,2,1,256,256]{4,3,2,1,0:T(8,128)(2,1)} %param.14) | copy-start | bytes 1572868
  51.0 7.1 %copy-start.2 = (s32[2,2]{1,0:T(2,128)S(1)}, s32[2,2]{1,0:T(2,128)}, u32[]{:S(2)}) copy-start(s32[2,2]{1,0:T(2,128)} %param.17) | copy-start | bytes 52
  51.0 8.3 %copy-start.1 = (s32[2,2,16]{2,1,0:T(2,128)S(1)}, s32[2,2,16]{2,1,0:T(2,128)}, u32[]{:S(2)}) copy-start(s32[2,2,16]{2,1,0:T(2,128)} %param.16) | copy-start | bytes 772
  51.0 131.0 %all-to-all-start = ((bf16[16,256,512]{2,1,0:T(8,128)(2,1)}), bf16[16,256,512]{2,1,0:T(8,128)(2,1)}, u32[]{:S(2)}, u32[]{:S(2)}) async-start(bf16[16,256,512]{2,1,0:T(8,128)(2,1)} %broadcast_select_fusion.1), calls=%async_computation | async-start | bytes 8388608 | tf_op jit(solution)/shard_map/all_to_all | solution.py:47
  57.2 124.8 %all-gather.8.cloned.1.call-start = ((), (), s32[]{:S(2)}) async-start(), calls=%async_computation.2 | async-start | bytes 4456448 | tf_op jit(solution)/shard_map/all_gather | solution.py:41
  251.4 138.2 %all-to-all-start.1 = ((bf16[16,256,512]{2,1,0:T(8,128)(2,1)}), bf16[16,256,512]{2,1,0:T(8,128)(2,1)}, u32[]{:S(2)}, u32[]{:S(2)}) async-start(bf16[16,256,512]{2,1,0:T(8,128)(2,1)} %broadcast_select_fusion), calls=%async_computation.1 | async-start | bytes 8388608 | tf_op jit(solution)/shard_map/all_to_all | solution.py:47
  266.2 130.8 %all-gather.10.cloned.1.call-start = ((), (), s32[]{:S(2)}) async-start(), calls=%async_computation.3 | async-start | bytes 4456448 | tf_op jit(solution)/shard_map/all_gather | solution.py:41
Sparse Core Ops, SparseCore 0:
  60.8 112.7 all-gather.7
  269.8 111.0 all-gather.9
where the time goes:
time: 499 us; the launch traced here: 495 us
  blocking collectives  229 us (46%)
  local copies, waits for them, and re-layouts  111 us (22%)
  waiting for transfers between devices  49.7 us (10%)
  matrix products  48.1 us (10%)
  starting transfers between devices  21.1 us (4%)
  other arithmetic  19.4 us (4%)
  between operations  14.7 us (3%)
    all_gather x3, blocking collectives, apply_inverse(): lax.all_gather(inverse_part, 'draw', axis=1, tiled=True)  229 us
    gather x30, local copies, waits for them, and re-layouts, turn(): picked = jnp.take(table, wanted, axis=0)  102 us
    all_to_all x2, waiting for transfers between devices, share_level(): lax.all_to_all(outgoing, 'leaf', split_axis=0, concat_axis=0, tiled=True)  49 us
    dot_general x30, matrix products, turn(): jnp.einsum('nrc,nrs->ncs', block, picked, preferred_element_type=jnp.floa...  44 us
    all_to_all x2, starting transfers between devices, share_level(): lax.all_to_all(outgoing, 'leaf', split_axis=0, concat_axis=0, tiled=True)  21 us
  transfers between devices with their start and end apart: 4, of which 2 were waited for; matrix products, arithmetic and copies ran while one was open for 2% of the time, Pallas kernels for 0%

commit v1 on v0

v1 whole, which is shorter than its diff:
```python
import jax
import jax.numpy as jnp
from jax import lax
from jax.experimental import pallas as pl
from jax.experimental.pallas import tpu as pltpu
from jax.sharding import PartitionSpec as P

MESH = pl.DeviceIdType.MESH
YS, ZS, XS, CORES = 4, 4, 4, 2
RING = 2 * ZS
DRAWS = 2 * XS * CORES
W = 256
F32, BF16 = jnp.float32, jnp.bfloat16


def kernel(pick, lists, counts, noise, inverse, blocks, out, *scratch):
    (noise_v, out_v, i0, i12, b1, b2, zrel, own0, own1, below, above, t0, t1, sb0, sb1, ry0, ry1, acc) = scratch[:18]
    (loc, inv_s, inv_r, zs, zr, xs, xr, xfs, xfr, cs, cr, ls, lr_b, lr_a, ys, yr, yfs, yfr, yrel) = scratch[18:]
    cols = own0.shape[1]
    half = cols // 2
    bf, own, table, send, relay = (b1, b2), (own0, own1), (t0, t1), (sb0, sb1), (ry0, ry1)
    below = (below[:3], below[3:])
    above = (above[:3], above[3:])

    leaf, draw = lax.axis_index("leaf"), lax.axis_index("draw")
    y, zl = lax.div(leaf, ZS), lax.rem(leaf, ZS)
    zh, q = lax.div(draw, XS * CORES), lax.rem(draw, XS * CORES)
    x, c = lax.div(q, CORES), lax.rem(q, CORES)
    z = zh * ZS + zl

    def at(y_, z_, x_, c_):
        return (y_ * ZS + lax.rem(z_, ZS), lax.div(z_, ZS) * (XS * CORES) + x_ * CORES + c_)

    def up(v, step, size):
        return lax.rem(v + step + size, size)

    north, south = at(up(y, 1, YS), z, x, c), at(up(y, -1, YS), z, x, c)
    z_up, z_down = at(y, up(z, 1, RING), x, c), at(y, up(z, -1, RING), x, c)
    z_up2, z_down2 = at(y, up(z, 2, RING), x, c), at(y, up(z, -2, RING), x, c)
    partner = at(y, up(z, ZS, RING), x, c)
    east, west = at(y, z, up(x, 1, XS), c), at(y, z, up(x, -1, XS), c)
    other = at(y, z, x, 1 - c)

    def slot(zh_, x_, c_):
        return zh_ * (XS * CORES) + x_ * CORES + c_

    pending = []

    def move(src, dst, s_sem, r_sem, device):
        return pltpu.make_async_remote_copy(
            src_ref=src, dst_ref=dst, send_sem=s_sem, recv_sem=r_sem, device_id=device, device_id_type=MESH
        )

    def put(*args, cond=None):
        if cond is None:
            move(*args).start()
        else:
            pl.when(cond)(lambda: move(*args).start())
        pending.append((args, cond))

    def got(dst, r_sem):
        move(dst, dst, r_sem, r_sem, east).wait_recv()

    def run(plan, cond=None):
        def body():
            for step in plan:
                if len(step) == 2:
                    got(*step)
                else:
                    move(*step).start()

        if cond is None:
            body()
        else:
            pl.when(cond)(body)
        pending.extend((step, cond) for step in plan if len(step) == 5)

    barrier = pltpu.get_barrier_semaphore()
    peers = [(leaf, zh * (XS * CORES) + lax.rem(q + j, XS * CORES)) for j in range(1, XS * CORES)]
    greeted = peers + [partner, z_up, z_down, z_up2, z_down2, north, south]
    noise_in = pltpu.make_async_copy(noise, noise_v, loc.at[0])
    noise_in.start()
    for device in greeted:
        pl.semaphore_signal(barrier, inc=1, device_id=device, device_id_type=MESH)
    pl.semaphore_wait(barrier, len(greeted))

    inv_dst = (
        lambda k: i0.at[:, pl.ds(pl.multiple_of(16 * k, 16), 16), :],
        lambda k: i12.at[:, :, pl.ds(pl.multiple_of(16 * k, 16), 16), :],
    )
    inv_src = (inverse.at[0], inverse.at[pl.ds(1, 2)])
    far = lax.rem(draw + XS * CORES, DRAWS)

    def inverse_first(g):
        put(inv_src[g], inv_dst[g](draw), inv_s.at[g, 0], inv_r.at[g, draw], partner)
        for j, device in enumerate(peers):
            put(inv_src[g], inv_dst[g](draw), inv_s.at[g, 1 + j], inv_r.at[g, draw], device)

    def inverse_next(g):
        got(inv_dst[g](far), inv_r.at[g, far])
        for j, device in enumerate(peers):
            put(inv_dst[g](far), inv_dst[g](far), inv_s.at[g, 8 + j], inv_r.at[g, far], device)

    def inverse_wait(g):
        for j in range(1, XS * CORES):
            for zz in (0, 1):
                k = zz * (XS * CORES) + lax.rem(q + j, XS * CORES)
                got(inv_dst[g](k), inv_r.at[g, k])

    inverse_own = [pltpu.make_async_copy(inv_src[g], inv_dst[g](draw), loc.at[1 + g]) for g in (0, 1)]
    blocks_own = [pltpu.make_async_copy(blocks.at[l, :, 0], bf[l].at[draw], loc.at[3 + l]) for l in (0, 1)]

    def blocks_z(l):
        put(blocks.at[l, 0, 0], zrel.at[l, 0], zs.at[l, 0], zr.at[l, 0], z_up2)
        put(blocks.at[l, 1, 0], zrel.at[l, 1], zs.at[l, 1], zr.at[l, 1], z_down2)

    def blocks_relay(l):
        k_up = slot(lax.div(up(z, -2, RING), ZS), x, c)
        k_down = slot(lax.div(up(z, 2, RING), ZS), x, c)
        got(zrel.at[l, 0], zr.at[l, 0])
        put(zrel.at[l, 0], bf[l].at[k_up, 0], zs.at[l, 2], zr.at[l, 2], z_up2)
        got(zrel.at[l, 1], zr.at[l, 1])
        put(zrel.at[l, 1], bf[l].at[k_down, 1], zs.at[l, 3], zr.at[l, 3], z_down2)

    def blocks_out(l, u):
        k = (draw, far)[u]
        src = blocks.at[l, :, 0] if u == 0 else bf[l].at[k]
        put(src, bf[l].at[k], xs.at[l, u, 0], xr.at[l, u, 0], east)
        put(src, bf[l].at[k], xs.at[l, u, 1], xr.at[l, u, 1], west)
        put(src, bf[l].at[k], cs.at[l, u, 0], cr.at[l, u, 0], other)

    def blocks_far(l):
        got(bf[l].at[far, 0], zr.at[l, 2])
        got(bf[l].at[far, 1], zr.at[l, 3])
        blocks_out(l, 1)

    def blocks_x(l, u):
        zz = zh if u == 0 else 1 - zh
        k_w, k_e = slot(zz, up(x, -1, XS), c), slot(zz, up(x, 1, XS), c)
        got(bf[l].at[k_w], xr.at[l, u, 0])
        put(bf[l].at[k_w, 0], bf[l].at[k_w, 0], xfs.at[l, u, 0], xfr.at[l, u, 0], east)
        put(bf[l].at[k_w], bf[l].at[k_w], cs.at[l, u, 1], cr.at[l, u, 1], other)
        got(bf[l].at[k_e], xr.at[l, u, 1])
        put(bf[l].at[k_e, 1], bf[l].at[k_e, 1], xfs.at[l, u, 1], xfr.at[l, u, 1], west)
        put(bf[l].at[k_e], bf[l].at[k_e], cs.at[l, u, 2], cr.at[l, u, 2], other)

    def blocks_x2(l, u):
        k = slot(zh if u == 0 else 1 - zh, up(x, 2, XS), c)
        for n in (0, 1):
            got(bf[l].at[k, n], xfr.at[l, u, n])
            put(bf[l].at[k, n], bf[l].at[k, n], cs.at[l, u, 3 + n], cr.at[l, u, 3 + n], other)

    def blocks_wait(l):
        for u in (0, 1):
            zz = zh if u == 0 else 1 - zh
            for i, step in enumerate((0, -1, 1)):
                k = slot(zz, up(x, step, XS), 1 - c)
                got(bf[l].at[k], cr.at[l, u, i])
            k = slot(zz, up(x, 2, XS), 1 - c)
            for n in (0, 1):
                got(bf[l].at[k, n], cr.at[l, u, 3 + n])
        blocks_own[l].wait()

    def choose(a, ref, s):
        src = y * ZS + s

        def wanted(step):
            return ref[pick[a, up(y, step, YS) * ZS + zl, src]]

        send[a][s, 0] = wanted(2)
        send[a][s, 1] = wanted(1)
        send[a][s, 2] = wanted(-1)
        table[a][src] = wanted(0)

    def send_y(a, s):
        src = y * ZS + s
        return [
            (send[a].at[s, 0, pl.ds(0, half)], relay[a].at[0, s], ys.at[a, s, 0], yrel.at[a, 0, s], north),
            (send[a].at[s, 0, pl.ds(half, half)], relay[a].at[1, s], ys.at[a, s, 1], yrel.at[a, 1, s], south),
            (send[a].at[s, 1], table[a].at[src], ys.at[a, s, 2], yr.at[a, 0, s], north),
            (send[a].at[s, 2], table[a].at[src], ys.at[a, s, 3], yr.at[a, 1, s], south),
        ]

    def pass_y(a, s):
        src0, src1 = up(y, -1, YS) * ZS + s, up(y, 1, YS) * ZS + s
        return [
            (relay[a].at[0, s], yrel.at[a, 0, s]),
            (relay[a].at[0, s], table[a].at[src0, pl.ds(0, half)], yfs.at[a, s, 0], yfr.at[a, 0, s], north),
            (relay[a].at[1, s], yrel.at[a, 1, s]),
            (relay[a].at[1, s], table[a].at[src1, pl.ds(half, half)], yfs.at[a, s, 1], yfr.at[a, 1, s], south),
        ]

    def arrived(a, s):
        got(table[a].at[up(y, -1, YS) * ZS + s], yr.at[a, 0, s])
        got(table[a].at[up(y, 1, YS) * ZS + s], yr.at[a, 1, s])
        k = up(y, 2, YS) * ZS + s
        got(table[a].at[k, pl.ds(0, half)], yfr.at[a, 0, s])
        got(table[a].at[k, pl.ds(half, half)], yfr.at[a, 1, s])

    def round_first(a):
        choose(a, own[a], zl)
        put(own[a], below[a][0], ls.at[a, 0, 0], lr_b.at[a, 0], z_up, cond=zl < ZS - 1)
        put(own[a], above[a][0], ls.at[a, 1, 0], lr_a.at[a, 0], z_down, cond=zl > 0)
        run(send_y(a, zl))

    def round_next(a, r):
        lines = (
            (below, lr_b, 0, z_up, zl >= r, zl < ZS - 1, zl - r),
            (above, lr_a, 1, z_down, zl <= ZS - 1 - r, zl > 0, zl + r),
        )
        for line, heard, way, device, here, more, s in lines:
            run([(line[a][r - 1], heard.at[a, r - 1])], here)
            if r < ZS - 1:
                put(
                    line[a][r - 1], line[a][r], ls.at[a, way, r], heard.at[a, r], device,
                    cond=jnp.logical_and(here, more),
                )
        for line, heard, way, device, here, more, s in lines:
            pl.when(here)(lambda line=line, s=s: choose(a, line[a][r - 1], s))
            run(send_y(a, s), here)

    def round_pass(a, r):
        if r == 0:
            run(pass_y(a, zl))
        else:
            run(pass_y(a, zl - r), zl >= r)
            run(pass_y(a, zl + r), zl <= ZS - 1 - r)

    def solve(level, right_side, n):
        inv = i0[n] if level == 0 else i12[level - 1, n]
        return jnp.dot(right_side, inv, preferred_element_type=F32).astype(BF16)

    def show(level, ref):
        for n in (0, 1):
            out_v[level, n] = ref[n].T
        copy = pltpu.make_async_copy(out_v.at[level], out.at[level], loc.at[5 + level])
        copy.start()
        return copy

    def add_slots(level, start, stop, source):
        @pl.loop(start, stop)
        def _(k):
            for n in (0, 1):
                alive = (k < counts[level, n]).astype(F32)
                values = source[lax.rem(lists[level, n, k], 16)]
                acc[n] += alive * jnp.dot(values, bf[level][k, n], preferred_element_type=F32)

    for copy in inverse_own + blocks_own:
        copy.start()
    inverse_first(0)
    blocks_z(0)
    noise_in.wait()
    flipped = [noise_v[0, n].T for n in (0, 1)]
    inverse_next(0)
    blocks_out(0, 0)
    inverse_own[0].wait()
    inverse_wait(0)
    for n in (0, 1):
        own0[n] = solve(0, flipped[n], n)
    round_first(0)
    inverse_first(1)
    blocks_relay(0)
    blocks_x(0, 0)
    blocks_far(0)
    shown = [show(0, own0)]
    round_next(0, 1)
    round_pass(0, 0)
    blocks_x(0, 1)
    blocks_x2(0, 0)
    inverse_next(1)
    round_next(0, 2)
    round_pass(0, 1)
    blocks_x2(0, 1)
    blocks_z(1)
    blocks_out(1, 0)
    round_next(0, 3)
    round_pass(0, 2)
    round_pass(0, 3)
    blocks_relay(1)
    blocks_wait(0)
    inverse_own[1].wait()
    inverse_wait(1)

    for n in (0, 1):
        acc[n] = jnp.zeros_like(acc[n])
    for s in range(ZS):
        arrived(0, s)
    add_slots(0, 0, 16, t0)
    for n in (0, 1):
        right_side = (noise_v[1, n].T.astype(F32) - acc[n]).astype(BF16)
        own1[n] = solve(1, right_side, n)
    round_first(1)
    blocks_x(1, 0)
    blocks_far(1)
    shown.append(show(1, own1))
    for n in (0, 1):
        acc[n] = jnp.zeros_like(acc[n])
    round_next(1, 1)
    round_pass(1, 0)
    blocks_x(1, 1)
    blocks_x2(1, 0)
    round_next(1, 2)
    round_pass(1, 1)
    blocks_x2(1, 1)
    round_next(1, 3)
    round_pass(1, 2)
    blocks_wait(1)
    add_slots(1, 8, 16, t0)
    round_pass(1, 3)

    for s in range(ZS):
        arrived(1, s)
    add_slots(1, 0, 8, t1)
    for n in (0, 1):
        right_side = (noise_v[2, n].T.astype(F32) - acc[n]).astype(BF16)
        out_v[2, n] = solve(2, right_side, n).T
    last = pltpu.make_async_copy(out_v.at[2], out.at[2], loc.at[7])
    last.start()
    for args, cond in pending:
        if cond is None:
            move(*args).wait_send()
        else:
            pl.when(cond)(lambda args=args: move(*args).wait_send())
    for copy in shown + [last]:
        copy.wait()


def on_device(noise_draws, inverse_diagonal, coupling_blocks, ancestor_pick, coupling_lists, live_counts):
    cols = noise_draws.shape[3]
    pair = pltpu.VMEM((2, cols, W), BF16)
    dma = pltpu.SemaphoreType.DMA
    scratch = [
        pltpu.VMEM(noise_draws.shape, BF16),
        pltpu.VMEM(noise_draws.shape, BF16),
        pltpu.VMEM((2, W, W), BF16),
        pltpu.VMEM((2, 2, W, W), BF16),
        pltpu.VMEM((DRAWS, 2, W, W), BF16),
        pltpu.VMEM((DRAWS, 2, W, W), BF16),
        pltpu.VMEM((2, 2, W, W), BF16),
        pair,
        pair,
        [pair] * 6,
        [pair] * 6,
        pltpu.VMEM((16, cols, W), BF16),
        pltpu.VMEM((16, cols, W), BF16),
        pltpu.VMEM((ZS, 3, cols, W), BF16),
        pltpu.VMEM((ZS, 3, cols, W), BF16),
        pltpu.VMEM((2, ZS, cols // 2, W), BF16),
        pltpu.VMEM((2, ZS, cols // 2, W), BF16),
        pltpu.VMEM((2, cols, W), F32),
        dma((8,)),
        dma((2, 16)),
        dma((2, 16)),
        dma((2, 4)),
        dma((2, 4)),
        dma((2, 2, 2)),
        dma((2, 2, 2)),
        dma((2, 2, 2)),
        dma((2, 2, 2)),
        dma((2, 2, 5)),
        dma((2, 2, 5)),
        dma((2, 2, 3)),
        dma((2, 3)),
        dma((2, 3)),
        dma((2, ZS, 4)),
        dma((2, 2, ZS)),
        dma((2, ZS, 2)),
        dma((2, 2, ZS)),
        dma((2, 2, ZS)),
    ]
    smem = pl.BlockSpec(memory_space=pltpu.SMEM)
    anywhere = pl.BlockSpec(memory_space=pl.ANY)
    return pl.pallas_call(
        kernel,
        out_shape=jax.ShapeDtypeStruct(noise_draws.shape, BF16),
        in_specs=[smem, smem, smem, anywhere, anywhere, anywhere],
        out_specs=anywhere,
        scratch_shapes=scratch,
        compiler_params=pltpu.CompilerParams(
            collective_id=0, has_side_effects=True, vmem_limit_bytes=60 * 1024 * 1024
        ),
    )(ancestor_pick, coupling_lists, live_counts, noise_draws, inverse_diagonal, coupling_blocks)


def solution(mesh):
    placed = (
        P(None, "leaf", None, "draw"),
        P(None, "leaf", "draw", None),
        P(None, "leaf", "draw", None, None),
        P(),
        P(None, "leaf", None),
        P(None, "leaf"),
    )
    return jax.shard_map(
        on_device,
        mesh=mesh,
        in_specs=placed,
        out_specs=P(None, "leaf", None, "draw"),
        check_vma=False,
    )
```

time: 499 us -> 144 us (0.29)
  the two profiles are of different devices: /device:TPU:24 before, /device:TPU:1 now
where the time goes in v1:
time: 144 us; the launch traced here: 143 us
  Pallas kernels  140 us (97%)
  local copies, waits for them, and re-layouts  2.74 us (2%)
    pallas_call x1, Pallas kernels, on_device(): pl.pallas_call(kernel, out_shape=jax.ShapeDtypeStruct(noise_draws.shape,...  140 us

profile of v1, /device:TPU:1, one launch (start us, length us, event | category | flops | bytes accessed | tf_op | source)
XLA Modules:
  0.0 142.8 jit_solution(13684387306027795897)
XLA Ops:
  0.0 140.1 %shard_map.64 = bf16[3,2,256,512]{3,2,1,0:T(8,128)(2,1)} custom-call(s32[2,16,16]{2,1,0:T(8,128)} %pick.1, s32[2,2,16]{2,1,0:T(2,128)} %lists.1, s32[2,2]{1,0:T(2,128)} %counts.1, bf16[3,2,256,512]{3,2,1,0:T(8,128)(2,1)} %noise.1, bf16[3,2,16,256]{3,2,1,0:T(8,128)(2,1)} %inverse.1, bf16[2,2,1,256,256]{4,3,2,1,0:T(8,128)(2,1)} %blocks.1), custom_call_target="tpu_custom_call" | custom-call | tf_op jit(solution)/shard_map/pallas_call | solution.py:373
  140.1 2.7 %copy.8 = bf16[3,2,256,512]{3,2,1,0:T(8,128)(2,1)} copy(bf16[3,2,256,512]{3,2,1,0:T(8,128)(2,1)} %shard_map.64) | data formatting | bytes 3145728

commit v2 on v1

v2 whole, which is shorter than its diff:
```python
import jax
import jax.numpy as jnp
from jax import lax
from jax.experimental import pallas as pl
from jax.experimental.pallas import tpu as pltpu
from jax.sharding import PartitionSpec as P

MESH = pl.DeviceIdType.MESH
YS, ZS, XS, CORES = 4, 4, 4, 2
RING = 2 * ZS
DRAWS = 2 * XS * CORES
OWNERS, SLOTS, W = 16, 16, 256
F32, BF16 = jnp.float32, jnp.bfloat16


def kernel(pick, lists, counts, noise, inverse, blocks, out_v, *scratch):
    (noise_v, flipped, i0, i12, b1, b2, zrel, own0, own1, below, above, t0, t1, sb0, sb1, ry0, ry1, acc, place) = scratch[:19]
    (loc, inv_s, inv_r, zs, zr, xs, xr, xfs, xfr, cs, cr, ls, lr, ys, yr, yrel) = scratch[19:]
    cols = own0.shape[1]
    half = cols // 2
    bf, own, table, send, relay = (b1, b2), (own0, own1), (t0, t1), (sb0, sb1), (ry0, ry1)

    leaf, draw = lax.axis_index("leaf"), lax.axis_index("draw")
    y, zl = lax.div(leaf, ZS), lax.rem(leaf, ZS)
    zh, q = lax.div(draw, XS * CORES), lax.rem(draw, XS * CORES)
    x, c = lax.div(q, CORES), lax.rem(q, CORES)
    z = zh * ZS + zl

    def at(y_, z_, x_, c_):
        return (y_ * ZS + lax.rem(z_, ZS), lax.div(z_, ZS) * (XS * CORES) + x_ * CORES + c_)

    def up(v, step, size):
        return lax.rem(v + step + size, size)

    north, south = at(up(y, 1, YS), z, x, c), at(up(y, -1, YS), z, x, c)
    z_up, z_down = at(y, up(z, 1, RING), x, c), at(y, up(z, -1, RING), x, c)
    z_up2, z_down2 = at(y, up(z, 2, RING), x, c), at(y, up(z, -2, RING), x, c)
    partner = at(y, up(z, ZS, RING), x, c)
    east, west = at(y, z, up(x, 1, XS), c), at(y, z, up(x, -1, XS), c)
    other = at(y, z, x, 1 - c)

    def slot(zh_, x_, c_):
        return zh_ * (XS * CORES) + x_ * CORES + c_

    pending = []

    def move(src, dst, s_sem, r_sem, device):
        return pltpu.make_async_remote_copy(
            src_ref=src, dst_ref=dst, send_sem=s_sem, recv_sem=r_sem, device_id=device, device_id_type=MESH
        )

    def put(*args, cond=None):
        if cond is None:
            move(*args).start()
        else:
            pl.when(cond)(lambda: move(*args).start())
        pending.append((args, cond))

    def got(dst, r_sem):
        move(dst, dst, r_sem, r_sem, east).wait_recv()

    def run(plan, cond=None):
        def body():
            for step in plan:
                if len(step) == 2:
                    got(*step)
                else:
                    move(*step).start()

        if cond is None:
            body()
        else:
            pl.when(cond)(body)
        pending.extend((step, cond) for step in plan if len(step) == 5)

    barrier = pltpu.get_barrier_semaphore()
    peers = [(leaf, zh * (XS * CORES) + lax.rem(q + j, XS * CORES)) for j in range(1, XS * CORES)]
    greeted = peers + [partner, z_up, z_down, z_up2, z_down2, north, south]
    noise_in = pltpu.make_async_copy(noise, noise_v, loc.at[0])
    noise_in.start()
    for device in greeted:
        pl.semaphore_signal(barrier, inc=1, device_id=device, device_id_type=MESH)
    pl.semaphore_wait(barrier, len(greeted))

    inv_dst = (
        lambda k: i0.at[:, pl.ds(pl.multiple_of(16 * k, 16), 16), :],
        lambda k: i12.at[:, :, pl.ds(pl.multiple_of(16 * k, 16), 16), :],
    )
    inv_src = (inverse.at[0], inverse.at[pl.ds(1, 2)])
    far = lax.rem(draw + XS * CORES, DRAWS)

    def inverse_across(g):
        put(inv_src[g], inv_dst[g](draw), inv_s.at[g, 0], inv_r.at[g, draw], partner)

    def inverse_first(g):
        for j, device in enumerate(peers):
            put(inv_src[g], inv_dst[g](draw), inv_s.at[g, 1 + j], inv_r.at[g, draw], device)

    def inverse_next(g):
        got(inv_dst[g](far), inv_r.at[g, far])
        for j, device in enumerate(peers):
            put(inv_dst[g](far), inv_dst[g](far), inv_s.at[g, 8 + j], inv_r.at[g, far], device)

    def inverse_wait(g):
        for j in range(1, XS * CORES):
            for zz in (0, 1):
                k = zz * (XS * CORES) + lax.rem(q + j, XS * CORES)
                got(inv_dst[g](k), inv_r.at[g, k])

    inverse_own = [pltpu.make_async_copy(inv_src[g], inv_dst[g](draw), loc.at[1 + g]) for g in (0, 1)]
    blocks_own = [pltpu.make_async_copy(blocks.at[l, :, 0], bf[l].at[draw], loc.at[3 + l]) for l in (0, 1)]

    def blocks_z(l):
        put(blocks.at[l, 0, 0], zrel.at[l, 0], zs.at[l, 0], zr.at[l, 0], z_up2)
        put(blocks.at[l, 1, 0], zrel.at[l, 1], zs.at[l, 1], zr.at[l, 1], z_down2)

    def blocks_relay(l):
        k_up = slot(lax.div(up(z, -2, RING), ZS), x, c)
        k_down = slot(lax.div(up(z, 2, RING), ZS), x, c)
        got(zrel.at[l, 0], zr.at[l, 0])
        put(zrel.at[l, 0], bf[l].at[k_up, 0], zs.at[l, 2], zr.at[l, 2], z_up2)
        got(zrel.at[l, 1], zr.at[l, 1])
        put(zrel.at[l, 1], bf[l].at[k_down, 1], zs.at[l, 3], zr.at[l, 3], z_down2)

    def blocks_out(l, u):
        k = (draw, far)[u]
        src = blocks.at[l, :, 0] if u == 0 else bf[l].at[k]
        put(src, bf[l].at[k], xs.at[l, u, 0], xr.at[l, u, 0], east)
        put(src, bf[l].at[k], xs.at[l, u, 1], xr.at[l, u, 1], west)
        put(src, bf[l].at[k], cs.at[l, u, 0], cr.at[l, u, 0], other)

    def blocks_far(l):
        got(bf[l].at[far, 0], zr.at[l, 2])
        got(bf[l].at[far, 1], zr.at[l, 3])
        blocks_out(l, 1)

    def blocks_x(l, u):
        zz = zh if u == 0 else 1 - zh
        k_w, k_e = slot(zz, up(x, -1, XS), c), slot(zz, up(x, 1, XS), c)
        got(bf[l].at[k_w], xr.at[l, u, 0])
        put(bf[l].at[k_w, 0], bf[l].at[k_w, 0], xfs.at[l, u, 0], xfr.at[l, u, 0], east)
        put(bf[l].at[k_w], bf[l].at[k_w], cs.at[l, u, 1], cr.at[l, u, 1], other)
        got(bf[l].at[k_e], xr.at[l, u, 1])
        put(bf[l].at[k_e, 1], bf[l].at[k_e, 1], xfs.at[l, u, 1], xfr.at[l, u, 1], west)
        put(bf[l].at[k_e], bf[l].at[k_e], cs.at[l, u, 2], cr.at[l, u, 2], other)

    def blocks_x2(l, u):
        k = slot(zh if u == 0 else 1 - zh, up(x, 2, XS), c)
        for n in (0, 1):
            got(bf[l].at[k, n], xfr.at[l, u, n])
            put(bf[l].at[k, n], bf[l].at[k, n], cs.at[l, u, 3 + n], cr.at[l, u, 3 + n], other)

    def blocks_wait(l):
        for u in (0, 1):
            zz = zh if u == 0 else 1 - zh
            for i, step in enumerate((0, -1, 1)):
                k = slot(zz, up(x, step, XS), 1 - c)
                got(bf[l].at[k], cr.at[l, u, i])
            k = slot(zz, up(x, 2, XS), 1 - c)
            for n in (0, 1):
                got(bf[l].at[k, n], cr.at[l, u, 3 + n])
        blocks_own[l].wait()

    def rows(h):
        return pl.ds(h * half, half)

    def choose(a, s, h, pair):
        src = y * ZS + s

        def wanted(step):
            return pair(pick[a, up(y, step, YS) * ZS + zl, src])

        send[a][s, 0, rows(h)] = wanted(2)
        send[a][s, 1, rows(h)] = wanted(1)
        send[a][s, 2, rows(h)] = wanted(-1)
        table[a][src, rows(h)] = wanted(0)

    def send_y(a, s, h):
        dst = table[a].at[y * ZS + s, rows(h)]
        far_way = (north, south)[h]
        return [
            (send[a].at[s, 0, rows(h)], relay[a].at[h, s], ys.at[a, s, h, 0], yrel.at[a, h, s], far_way),
            (send[a].at[s, 1, rows(h)], dst, ys.at[a, s, h, 1], yr.at[a, s, h, 0], north),
            (send[a].at[s, 2, rows(h)], dst, ys.at[a, s, h, 2], yr.at[a, s, h, 1], south),
        ]

    def pass_y(a, s, h):
        src = up(y, (-1, 1)[h], YS) * ZS + s
        return [
            (relay[a].at[h, s], yrel.at[a, h, s]),
            (relay[a].at[h, s], table[a].at[src, rows(h)], ys.at[a, s, h, 3], yr.at[a, s, h, 2], (north, south)[h]),
        ]

    def first(a, h):
        choose(a, zl, h, lambda n: own[a][n, rows(h)])
        put(own[a].at[:, rows(h)], below[a][0][h], ls.at[a, 0, 0, h], lr.at[a, 0, 0, h], z_up, cond=zl < ZS - 1)
        put(own[a].at[:, rows(h)], above[a][0][h], ls.at[a, 1, 0, h], lr.at[a, 1, 0, h], z_down, cond=zl > 0)
        run(send_y(a, zl, h))

    def follow(a, r, h):
        lines = (
            (below, 0, z_up, zl >= r, zl < ZS - 1, zl - r),
            (above, 1, z_down, zl <= ZS - 1 - r, zl > 0, zl + r),
        )
        for line, way, device, here, more, s in lines:
            run([(line[a][r - 1][h], lr.at[a, way, r - 1, h])], here)
            if r < ZS - 1:
                put(
                    line[a][r - 1][h], line[a][r][h], ls.at[a, way, r, h], lr.at[a, way, r, h], device,
                    cond=jnp.logical_and(here, more),
                )
        for line, way, device, here, more, s in lines:
            pl.when(here)(lambda line=line, s=s: choose(a, s, h, lambda n: line[a][r - 1][h][n]))
            run(send_y(a, s, h), here)

    def by_round(r, body):
        if r == 0:
            body(zl, None)
        else:
            body(zl - r, zl >= r)
            body(zl + r, zl <= ZS - 1 - r)

    def hand_on(a, r, h):
        by_round(r, lambda s, cond: run(pass_y(a, s, h), cond))

    def add_source(a, src):
        if a == 0:
            for n in (0, 1):
                k = place[0, n, src]
                alive = (k < counts[0, n]).astype(F32)
                acc[n] += alive * jnp.dot(t0[src], b1[k, n], preferred_element_type=F32)
        else:
            k = place[1, 0, src]
            second = place[1, 1, src]
            term = jnp.dot(t1[src], b2[k, second], preferred_element_type=F32)
            share = second.astype(F32)
            acc[0] += (1.0 - share) * term
            acc[1] += share * term

    def guarded(cond, body):
        if cond is None:
            body()
        else:
            pl.when(cond)(body)

    def use_near(a, r):
        def body(s, cond):
            def inner():
                add_source(a, y * ZS + s)
                for way, step in ((0, -1), (1, 1)):
                    src = up(y, step, YS) * ZS + s
                    for h in (0, 1):
                        got(table[a].at[src, rows(h)], yr.at[a, s, h, way])
                    add_source(a, src)

            guarded(cond, inner)

        by_round(r, body)

    def use_far(a, r):
        def body(s, cond):
            def inner():
                src = up(y, 2, YS) * ZS + s
                for h in (0, 1):
                    got(table[a].at[src, rows(h)], yr.at[a, s, h, 2])
                add_source(a, src)

            guarded(cond, inner)

        by_round(r, body)

    def find_places():
        @pl.loop(0, OWNERS)
        def _(o):
            zero = jnp.int32(0)
            for n in (0, 1):
                found = zero
                for k in range(SLOTS):
                    found = jnp.where(lists[0, n, k] == o, k, found)
                place[0, n, o] = found
            k0, n0 = zero, zero
            for k in range(SLOTS // 2):
                first_has, second_has = (lists[1, n, k] == OWNERS + o for n in (0, 1))
                k0 = jnp.where(jnp.logical_or(first_has, second_has), k, k0)
                n0 = jnp.where(second_has, 1, n0)
            place[1, 0, o], place[1, 1, o] = k0, n0

    def add_lower():
        @pl.loop(SLOTS // 2, SLOTS)
        def _(k):
            for n in (0, 1):
                alive = (k < counts[1, n]).astype(F32)
                values = t0[lax.rem(lists[1, n, k], OWNERS)]
                acc[n] += alive * jnp.dot(values, b2[k, n], preferred_element_type=F32)

    def solve(level, n, h):
        inv = i0[n] if level == 0 else i12[level - 1, n]
        right_side = flipped[level, n, rows(h)]
        if level > 0:
            right_side = (right_side.astype(F32) - acc[n, rows(h)]).astype(BF16)
        return jnp.dot(right_side, inv, preferred_element_type=F32).astype(BF16)

    def clear():
        for n in (0, 1):
            acc[n] = jnp.zeros_like(acc[n])

    def flip(level):
        for n in (0, 1):
            flipped[level, n] = noise_v[level, n].T

    def show(level, ref):
        for n in (0, 1):
            out_v[level, n] = ref[n].T

    def last(n, h):
        out_v[2, n, :, rows(h)] = solve(2, n, h).T

    def settle():
        for args, cond in pending:
            guarded(cond, lambda args=args: move(*args).wait_send())
        pending.clear()

    for copy in inverse_own + blocks_own:
        copy.start()
    inverse_across(0)
    inverse_first(0)
    inverse_across(1)
    blocks_z(0)
    noise_in.wait()
    flip(0)
    inverse_next(0)
    blocks_relay(0)
    inverse_own[0].wait()
    inverse_wait(0)
    for h in (0, 1):
        for n in (0, 1):
            own0[n, rows(h)] = solve(0, n, h)
        first(0, h)
    blocks_out(0, 0)
    find_places()
    inverse_first(1)
    follow(0, 1, 0)
    hand_on(0, 0, 0)
    blocks_x(0, 0)
    blocks_far(0)
    follow(0, 1, 1)
    hand_on(0, 0, 1)
    clear()
    flip(1)
    blocks_x2(0, 0)
    follow(0, 2, 0)
    blocks_x(0, 1)
    inverse_next(1)
    follow(0, 2, 1)
    hand_on(0, 1, 0)
    blocks_x2(0, 1)
    blocks_out(1, 0)
    hand_on(0, 1, 1)
    blocks_wait(0)
    use_near(0, 0)
    follow(0, 3, 0)
    hand_on(0, 2, 0)
    blocks_z(1)
    use_far(0, 0)
    use_near(0, 1)
    follow(0, 3, 1)
    hand_on(0, 2, 1)
    blocks_x(1, 0)
    hand_on(0, 3, 0)
    blocks_relay(1)
    use_far(0, 1)
    use_near(0, 2)
    hand_on(0, 3, 1)
    use_far(0, 2)
    inverse_own[1].wait()
    inverse_wait(1)
    blocks_x2(1, 0)
    use_near(0, 3)
    use_far(0, 3)

    for h in (0, 1):
        for n in (0, 1):
            own1[n, rows(h)] = solve(1, n, h)
        first(1, h)
    clear()
    show(0, own0)
    flip(2)
    follow(1, 1, 0)
    hand_on(1, 0, 0)
    show(1, own1)
    follow(1, 1, 1)
    hand_on(1, 0, 1)
    blocks_far(1)
    follow(1, 2, 0)
    follow(1, 2, 1)
    hand_on(1, 1, 0)
    blocks_x(1, 1)
    hand_on(1, 1, 1)
    follow(1, 3, 0)
    hand_on(1, 2, 0)
    blocks_x2(1, 1)
    blocks_wait(1)
    use_near(1, 0)
    follow(1, 3, 1)
    hand_on(1, 2, 1)
    use_far(1, 0)
    use_near(1, 1)
    hand_on(1, 3, 0)
    use_far(1, 1)
    use_near(1, 2)
    hand_on(1, 3, 1)
    add_lower()
    use_far(1, 2)
    settle()
    use_near(1, 3)
    use_far(1, 3)

    for n in (0, 1):
        for h in (0, 1):
            last(n, h)
    settle()


def on_device(noise_draws, inverse_diagonal, coupling_blocks, ancestor_pick, coupling_lists, live_counts):
    cols = noise_draws.shape[3]
    pair = pltpu.VMEM((2, cols, W), BF16)
    lines = [[[pltpu.VMEM((2, cols // 2, W), BF16)] * 2] * (ZS - 1)] * 2
    dma = pltpu.SemaphoreType.DMA
    scratch = [
        pltpu.VMEM(noise_draws.shape, BF16),
        pltpu.VMEM((3, 2, cols, W), BF16),
        pltpu.VMEM((2, W, W), BF16),
        pltpu.VMEM((2, 2, W, W), BF16),
        pltpu.VMEM((DRAWS, 2, W, W), BF16),
        pltpu.VMEM((DRAWS, 2, W, W), BF16),
        pltpu.VMEM((2, 2, W, W), BF16),
        pair,
        pair,
        lines,
        lines,
        pltpu.VMEM((16, cols, W), BF16),
        pltpu.VMEM((16, cols, W), BF16),
        pltpu.VMEM((ZS, 3, cols, W), BF16),
        pltpu.VMEM((ZS, 3, cols, W), BF16),
        pltpu.VMEM((2, ZS, cols // 2, W), BF16),
        pltpu.VMEM((2, ZS, cols // 2, W), BF16),
        pltpu.VMEM((2, cols, W), F32),
        pltpu.SMEM((2, 2, OWNERS), jnp.int32),
        dma((9,)),
        dma((2, 16)),
        dma((2, 16)),
        dma((2, 4)),
        dma((2, 4)),
        dma((2, 2, 2)),
        dma((2, 2, 2)),
        dma((2, 2, 2)),
        dma((2, 2, 2)),
        dma((2, 2, 5)),
        dma((2, 2, 5)),
        dma((2, 2, 3, 2)),
        dma((2, 2, 3, 2)),
        dma((2, ZS, 2, 4)),
        dma((2, ZS, 2, 3)),
        dma((2, 2, ZS)),
    ]
    smem = pl.BlockSpec(memory_space=pltpu.SMEM)
    anywhere = pl.BlockSpec(memory_space=pl.ANY)
    return pl.pallas_call(
        kernel,
        out_shape=pltpu.VMEM(noise_draws.shape, BF16),
        in_specs=[smem, smem, smem, anywhere, anywhere, anywhere],
        out_specs=pl.BlockSpec(memory_space=pltpu.VMEM),
        scratch_shapes=scratch,
        compiler_params=pltpu.CompilerParams(
            collective_id=0, has_side_effects=True, vmem_limit_bytes=60 * 1024 * 1024
        ),
    )(ancestor_pick, coupling_lists, live_counts, noise_draws, inverse_diagonal, coupling_blocks)


def solution(mesh):
    placed = (
        P(None, "leaf", None, "draw"),
        P(None, "leaf", "draw", None),
        P(None, "leaf", "draw", None, None),
        P(),
        P(None, "leaf", None),
        P(None, "leaf"),
    )
    return jax.shard_map(
        on_device,
        mesh=mesh,
        in_specs=placed,
        out_specs=P(None, "leaf", None, "draw"),
        check_vma=False,
    )
```

time: 144 us -> 127 us (0.88)
  Pallas kernels: 140 us -> 123 us
  local copies, waits for them, and re-layouts: 2.74 us -> 1.15 us
    pallas_call x1, Pallas kernels: 140 us -> 123 us  [on_device(): pl.pallas_call(kernel, out_shape=pltpu.VMEM(noise_draws.shape, BF16), in_...]
    unnamed x1, local copies, waits for them, and re-layouts: 2.74 us -> 1.15 us
where the time goes in v2:
time: 127 us; the launch traced here: 125 us
  Pallas kernels  123 us (97%)
    pallas_call x1, Pallas kernels, on_device(): pl.pallas_call(kernel, out_shape=pltpu.VMEM(noise_draws.shape, BF16), in_...  123 us

profile of v2, /device:TPU:1, one launch (start us, length us, event | category | flops | bytes accessed | tf_op | source)
XLA Modules:
  0.0 124.6 jit_solution(9271744165010958911)
XLA Ops:
  0.0 123.4 %shard_map.64 = bf16[3,2,256,512]{3,2,1,0:T(8,128)(2,1)S(1)} custom-call(s32[2,16,16]{2,1,0:T(8,128)} %pick.1, s32[2,2,16]{2,1,0:T(2,128)} %lists.1, s32[2,2]{1,0:T(2,128)} %counts.1, bf16[3,2,256,512]{3,2,1,0:T(8,128)(2,1)} %noise.1, bf16[3,2,16,256]{3,2,1,0:T(8,128)(2,1)} %inverse.1, bf16[2,2,1,256,256]{4,3,2,1,0:T(8,128)(2,1)} %blocks.1), custom_call_target="tpu_custom_call" | custom-call | tf_op jit(solution)/shard_map/pallas_call | solution.py:468
  123.4 1.1 copy.8

commit v3 on v2

v3 whole, which is shorter than its diff:
```python
import jax
import jax.numpy as jnp
from jax import lax
from jax.experimental import pallas as pl
from jax.experimental.pallas import tpu as pltpu
from jax.sharding import PartitionSpec as P

MESH = pl.DeviceIdType.MESH
YS, ZS, XS, CORES = 4, 4, 4, 2
RING = 2 * ZS
DRAWS = 2 * XS * CORES
LEVELS, OWNERS, SLOTS, W = 3, 16, 16, 256
F32, BF16 = jnp.float32, jnp.bfloat16


def kernel(pick, lists, counts, noise, inverse, blocks, out_v, *scratch):
    (noise_v, flipped, inv, b1, b2, zrel, own0, own1, below, above, t0, t1, sb0, sb1, ry0, ry1, acc, place) = scratch[:18]
    (loc, sent, inv_r, zr, xr, xfr, cr, lr, yr, yrel) = scratch[18:]
    cols = own0.shape[1]
    half = cols // 2
    bf, own, table, send, relay = (b1, b2), (own0, own1), (t0, t1), (sb0, sb1), (ry0, ry1)

    leaf, draw = lax.axis_index("leaf"), lax.axis_index("draw")
    y, zl = lax.div(leaf, ZS), lax.rem(leaf, ZS)
    zh, q = lax.div(draw, XS * CORES), lax.rem(draw, XS * CORES)
    x, c = lax.div(q, CORES), lax.rem(q, CORES)
    z = zh * ZS + zl

    def at(y_, z_, x_, c_):
        return (y_ * ZS + lax.rem(z_, ZS), lax.div(z_, ZS) * (XS * CORES) + x_ * CORES + c_)

    def up(v, step, size):
        return lax.rem(v + step + size, size)

    north, south = at(up(y, 1, YS), z, x, c), at(up(y, -1, YS), z, x, c)
    z_up, z_down = at(y, up(z, 1, RING), x, c), at(y, up(z, -1, RING), x, c)
    z_up2, z_down2 = at(y, up(z, 2, RING), x, c), at(y, up(z, -2, RING), x, c)
    partner = at(y, up(z, ZS, RING), x, c)
    east, west = at(y, z, up(x, 1, XS), c), at(y, z, up(x, -1, XS), c)
    other = at(y, z, x, 1 - c)

    def slot(zh_, x_, c_):
        return zh_ * (XS * CORES) + x_ * CORES + c_

    inside = jnp.logical_and(zl > 0, zl < ZS - 1)
    def move(src, dst, s_sem, r_sem, device):
        return pltpu.make_async_remote_copy(
            src_ref=src, dst_ref=dst, send_sem=s_sem, recv_sem=r_sem, device_id=device, device_id_type=MESH
        )

    def put(*args, cond=None):
        run([args], cond)

    def got(dst, r_sem):
        move(dst, dst, r_sem, r_sem, east).wait_recv()

    def left(group, region):
        move(region, region, sent.at[group], sent.at[group], east).wait_send()

    def run(plan, cond=None):
        def body():
            for step in plan:
                if len(step) == 2:
                    got(*step)
                else:
                    move(*step).start()

        if cond is None:
            body()
        else:
            pl.when(cond)(body)

    barrier = pltpu.get_barrier_semaphore()
    peers = [(leaf, zh * (XS * CORES) + lax.rem(q + j, XS * CORES)) for j in range(1, XS * CORES)]
    greeted = peers + [partner, z_up, z_down, z_up2, z_down2, north, south]
    noise_in = pltpu.make_async_copy(noise, noise_v, loc.at[0])
    noise_in.start()
    for device in greeted:
        pl.semaphore_signal(barrier, inc=1, device_id=device, device_id_type=MESH)
    pl.semaphore_wait(barrier, len(greeted))

    inv_dst = [
        lambda k, level=level: inv.at[level, :, pl.ds(pl.multiple_of(16 * k, 16), 16), :] for level in range(LEVELS)
    ]
    inv_src = [inverse.at[level] for level in range(LEVELS)]
    far = lax.rem(draw + XS * CORES, DRAWS)

    def inverse_across(g):
        put(inv_src[g], inv_dst[g](draw), sent.at[g], inv_r.at[g, 0], partner)

    def inverse_first(g):
        for device in peers:
            put(inv_src[g], inv_dst[g](draw), sent.at[g], inv_r.at[g, 1], device)

    def inverse_next(g):
        got(inv_dst[g](far), inv_r.at[g, 0])
        for device in peers:
            put(inv_dst[g](far), inv_dst[g](far), sent.at[g], inv_r.at[g, 1], device)

    def inverse_wait(g):
        got(inv.at[g, :, pl.ds(0, 224)], inv_r.at[g, 1])

    inverse_own = [pltpu.make_async_copy(inv_src[g], inv_dst[g](draw), loc.at[1 + g]) for g in range(LEVELS)]
    blocks_own = [pltpu.make_async_copy(blocks.at[l, :, 0], bf[l].at[draw], loc.at[4 + l]) for l in (0, 1)]

    def blocks_z(l):
        put(blocks.at[l, 0, 0], zrel.at[l, 0], sent.at[LEVELS + l], zr.at[l, 0], z_up2)
        put(blocks.at[l, 1, 0], zrel.at[l, 1], sent.at[LEVELS + l], zr.at[l, 1], z_down2)

    def blocks_relay(l, cond=None):
        k_up = slot(lax.div(up(z, -2, RING), ZS), x, c)
        k_down = slot(lax.div(up(z, 2, RING), ZS), x, c)
        plan = [
            (zrel.at[l, 0], zr.at[l, 0]),
            (zrel.at[l, 0], bf[l].at[k_up, 0], sent.at[LEVELS + l], zr.at[l, 2], z_up2),
            (zrel.at[l, 1], zr.at[l, 1]),
            (zrel.at[l, 1], bf[l].at[k_down, 1], sent.at[LEVELS + l], zr.at[l, 3], z_down2),
        ]
        run(plan, cond)

    def blocks_out(l, u):
        k = (draw, far)[u]
        src = blocks.at[l, :, 0] if u == 0 else bf[l].at[k]
        put(src, bf[l].at[k], sent.at[LEVELS + l], xr.at[l, u, 0], east)
        put(src, bf[l].at[k], sent.at[LEVELS + l], xr.at[l, u, 1], west)
        put(src, bf[l].at[k], sent.at[LEVELS + l], cr.at[l], other)

    def blocks_far(l):
        got(bf[l].at[far, 0], zr.at[l, 2])
        got(bf[l].at[far, 1], zr.at[l, 3])
        blocks_out(l, 1)

    def blocks_x(l, u):
        zz = zh if u == 0 else 1 - zh
        k_w, k_e = slot(zz, up(x, -1, XS), c), slot(zz, up(x, 1, XS), c)
        got(bf[l].at[k_w], xr.at[l, u, 0])
        put(bf[l].at[k_w, 0], bf[l].at[k_w, 0], sent.at[LEVELS + l], xfr.at[l, u, 0], east)
        put(bf[l].at[k_w], bf[l].at[k_w], sent.at[LEVELS + l], cr.at[l], other)
        got(bf[l].at[k_e], xr.at[l, u, 1])
        put(bf[l].at[k_e, 1], bf[l].at[k_e, 1], sent.at[LEVELS + l], xfr.at[l, u, 1], west)
        put(bf[l].at[k_e], bf[l].at[k_e], sent.at[LEVELS + l], cr.at[l], other)

    def blocks_x2(l, u):
        k = slot(zh if u == 0 else 1 - zh, up(x, 2, XS), c)
        for n in (0, 1):
            got(bf[l].at[k, n], xfr.at[l, u, n])
            put(bf[l].at[k, n], bf[l].at[k, n], sent.at[LEVELS + l], cr.at[l], other)

    def blocks_wait(l):
        got(bf[l].at[pl.ds(0, DRAWS // 2)], cr.at[l])
        blocks_own[l].wait()

    def parts(r):
        whole = [(0, half, 0), (half, half, 1)]
        return whole if r < ZS - 1 else whole[:1] + [(half, half // 2, 1), (half + half // 2, half // 2, 1)]

    def rows(part):
        return pl.ds(part[0], part[1])

    def relay_rows(part):
        return pl.ds(part[0] % half, part[1])

    def choose(a, s, part, pair):
        src = y * ZS + s

        def wanted(step):
            return pair(pick[a, up(y, step, YS) * ZS + zl, src])

        send[a][s, 0, rows(part)] = wanted(2)
        send[a][s, 1, rows(part)] = wanted(1)
        send[a][s, 2, rows(part)] = wanted(-1)
        table[a][src, rows(part)] = wanted(0)

    def send_y(a, s, i, part):
        dst = table[a].at[y * ZS + s, rows(part)]
        way = part[2]
        return [
            (
                send[a].at[s, 0, rows(part)], relay[a].at[way, s, relay_rows(part)], sent.at[LEVELS + 2 + a],
                yrel.at[a, i, s], (north, south)[way],
            ),
            (send[a].at[s, 1, rows(part)], dst, sent.at[LEVELS + 2 + a], yr.at[a, s, 0], north),
            (send[a].at[s, 2, rows(part)], dst, sent.at[LEVELS + 2 + a], yr.at[a, s, 1], south),
        ]

    def pass_y(a, s, i, part):
        way = part[2]
        src = up(y, (-1, 1)[way], YS) * ZS + s
        held = relay[a].at[way, s, relay_rows(part)]
        return [
            (held, yrel.at[a, i, s]),
            (held, table[a].at[src, rows(part)], sent.at[LEVELS + 2 + a], yr.at[a, s, 2], (north, south)[way]),
        ]

    def first(a, h):
        part = parts(0)[h]
        choose(a, zl, part, lambda n: own[a][n, rows(part)])
        put(own[a].at[:, rows(part)], below[a][0][h], sent.at[LEVELS + 4 + a], lr.at[a, 0, 0, h], z_up, cond=zl < ZS - 1)
        put(own[a].at[:, rows(part)], above[a][0][h], sent.at[LEVELS + 4 + a], lr.at[a, 1, 0, h], z_down, cond=zl > 0)
        run(send_y(a, zl, h, part))

    def follow(a, r, i):
        part = parts(r)[i]
        lines = (
            (below, 0, z_up, zl >= r, zl < ZS - 1, zl - r),
            (above, 1, z_down, zl <= ZS - 1 - r, zl > 0, zl + r),
        )
        for line, way, device, here, more, s in lines:
            held = line[a][r - 1][i]
            run([(held, lr.at[a, way, r - 1, i])], here)
            if r < ZS - 1:
                sends = []
                for j, (start, width, _) in enumerate(parts(r + 1)):
                    if part[0] <= start < part[0] + part[1]:
                        piece = held.at[:, pl.ds(start - part[0], width)]
                        sends.append((piece, line[a][r][j], sent.at[LEVELS + 4 + a], lr.at[a, way, r, j], device))
                run(sends, jnp.logical_and(here, more))
        for line, way, device, here, more, s in lines:
            pl.when(here)(lambda line=line, s=s: choose(a, s, part, lambda n: line[a][r - 1][i][n]))
            run(send_y(a, s, i, part), here)

    def by_round(r, body):
        if r == 0:
            body(zl, None)
        else:
            body(zl - r, zl >= r)
            body(zl + r, zl <= ZS - 1 - r)

    def hand_on(a, r, i):
        by_round(r, lambda s, cond: run(pass_y(a, s, i, parts(r)[i]), cond))

    def add_source(a, src):
        if a == 0:
            for n in (0, 1):
                k = place[0, n, src]
                alive = (k < counts[0, n]).astype(F32)
                acc[n] += alive * jnp.dot(t0[src], b1[k, n], preferred_element_type=F32)
        else:
            k = place[1, 0, src]
            second = place[1, 1, src]
            term = jnp.dot(t1[src], b2[k, second], preferred_element_type=F32)
            share = second.astype(F32)
            acc[0] += (1.0 - share) * term
            acc[1] += share * term

    def guarded(cond, body):
        if cond is None:
            body()
        else:
            pl.when(cond)(body)

    def use_near(a, r):
        def body(s, cond):
            def inner():
                add_source(a, y * ZS + s)
                for way, step in ((0, -1), (1, 1)):
                    src = up(y, step, YS) * ZS + s
                    got(table[a].at[src], yr.at[a, s, way])
                    add_source(a, src)

            guarded(cond, inner)

        by_round(r, body)

    def use_far(a, r):
        def body(s, cond):
            def inner():
                src = up(y, 2, YS) * ZS + s
                got(table[a].at[src], yr.at[a, s, 2])
                add_source(a, src)

            guarded(cond, inner)

        by_round(r, body)

    def find_places():
        @pl.loop(0, OWNERS)
        def _(o):
            zero = jnp.int32(0)
            for n in (0, 1):
                found = zero
                for k in range(SLOTS):
                    found = jnp.where(lists[0, n, k] == o, k, found)
                place[0, n, o] = found
            k0, n0 = zero, zero
            for k in range(SLOTS // 2):
                first_has, second_has = (lists[1, n, k] == OWNERS + o for n in (0, 1))
                k0 = jnp.where(jnp.logical_or(first_has, second_has), k, k0)
                n0 = jnp.where(second_has, 1, n0)
            place[1, 0, o], place[1, 1, o] = k0, n0

    def add_lower():
        @pl.loop(SLOTS // 2, SLOTS)
        def _(k):
            for n in (0, 1):
                alive = (k < counts[1, n]).astype(F32)
                values = t0[lax.rem(lists[1, n, k], OWNERS)]
                acc[n] += alive * jnp.dot(values, b2[k, n], preferred_element_type=F32)

    def solve(level, n, part):
        right_side = flipped[level, n, rows(part)]
        if level > 0:
            right_side = (right_side.astype(F32) - acc[n, rows(part)]).astype(BF16)
        return jnp.dot(right_side, inv[level, n], preferred_element_type=F32).astype(BF16)

    def clear():
        for n in (0, 1):
            acc[n] = jnp.zeros_like(acc[n])

    def flip(level):
        for n in (0, 1):
            flipped[level, n] = noise_v[level, n].T

    def show(level, ref):
        for n in (0, 1):
            out_v[level, n] = ref[n].T

    def last(n):
        out_v[2, n] = solve(2, n, (0, cols)).T

    def settle(a):
        left(a, inv.at[a, :, pl.ds(0, 240)])
        left(LEVELS + a, table[a])
        left(LEVELS + 2 + a, table[a])
        pl.when(inside)(lambda: left(LEVELS + 4 + a, table[a].at[pl.ds(0, 10)]))
        pl.when(jnp.logical_not(inside))(lambda: left(LEVELS + 4 + a, table[a].at[pl.ds(0, 2)]))

    for copy in inverse_own + blocks_own:
        copy.start()
    inverse_across(0)
    inverse_first(0)
    blocks_z(0)
    inverse_across(1)
    noise_in.wait()
    flip(0)
    inverse_next(0)
    blocks_relay(0)
    inverse_own[0].wait()
    inverse_wait(0)
    for h in (0, 1):
        for n in (0, 1):
            own0[n, rows(parts(0)[h])] = solve(0, n, parts(0)[h])
        first(0, h)
    blocks_out(0, 0)
    find_places()
    inverse_first(1)
    follow(0, 1, 0)
    hand_on(0, 0, 0)
    blocks_x(0, 0)
    blocks_far(0)
    follow(0, 1, 1)
    hand_on(0, 0, 1)
    clear()
    flip(1)
    blocks_x2(0, 0)
    follow(0, 2, 0)
    blocks_x(0, 1)
    inverse_next(1)
    follow(0, 2, 1)
    hand_on(0, 1, 0)
    blocks_x2(0, 1)
    blocks_out(1, 0)
    hand_on(0, 1, 1)
    blocks_wait(0)
    use_near(0, 0)
    follow(0, 3, 0)
    hand_on(0, 2, 0)
    use_far(0, 0)
    follow(0, 3, 1)
    use_near(0, 1)
    hand_on(0, 2, 1)
    follow(0, 3, 2)
    blocks_z(1)
    blocks_x(1, 0)
    hand_on(0, 3, 0)
    blocks_relay(1, inside)
    use_far(0, 1)
    use_near(0, 2)
    hand_on(0, 3, 1)
    hand_on(0, 3, 2)
    blocks_relay(1, jnp.logical_not(inside))
    use_far(0, 2)
    inverse_own[1].wait()
    inverse_wait(1)
    blocks_x2(1, 0)
    use_near(0, 3)
    use_far(0, 3)

    for h in (0, 1):
        for n in (0, 1):
            own1[n, rows(parts(0)[h])] = solve(1, n, parts(0)[h])
        first(1, h)
    clear()
    show(0, own0)
    flip(2)
    follow(1, 1, 0)
    hand_on(1, 0, 0)
    show(1, own1)
    follow(1, 1, 1)
    hand_on(1, 0, 1)
    follow(1, 2, 0)
    blocks_far(1)
    inverse_across(2)
    inverse_first(2)
    follow(1, 2, 1)
    hand_on(1, 1, 0)
    blocks_x(1, 1)
    hand_on(1, 1, 1)
    follow(1, 3, 0)
    hand_on(1, 2, 0)
    blocks_x2(1, 1)
    blocks_wait(1)
    add_lower()
    settle(0)
    follow(1, 3, 1)
    hand_on(1, 2, 1)
    use_near(1, 0)
    use_far(1, 0)
    follow(1, 3, 2)
    use_near(1, 1)
    hand_on(1, 3, 0)
    inverse_next(2)
    use_far(1, 1)
    use_near(1, 2)
    hand_on(1, 3, 1)
    hand_on(1, 3, 2)
    use_far(1, 2)
    use_near(1, 3)
    inverse_own[2].wait()
    inverse_wait(2)
    use_far(1, 3)

    for n in (0, 1):
        last(n)
    settle(1)
    left(2, inv.at[2, :, pl.ds(0, 240)])


def on_device(noise_draws, inverse_diagonal, coupling_blocks, ancestor_pick, coupling_lists, live_counts):
    cols = noise_draws.shape[3]
    pair = pltpu.VMEM((2, cols, W), BF16)
    whole, fine = (pltpu.VMEM((2, width, W), BF16) for width in (cols // 2, cols // 4))
    lines = [[[whole] * 2] * (ZS - 2) + [[whole, fine, fine]]] * 2
    dma = pltpu.SemaphoreType.DMA
    scratch = [
        pltpu.VMEM(noise_draws.shape, BF16),
        pltpu.VMEM((3, 2, cols, W), BF16),
        pltpu.VMEM((LEVELS, 2, W, W), BF16),
        pltpu.VMEM((DRAWS, 2, W, W), BF16),
        pltpu.VMEM((DRAWS, 2, W, W), BF16),
        pltpu.VMEM((2, 2, W, W), BF16),
        pair,
        pair,
        lines,
        lines,
        pltpu.VMEM((16, cols, W), BF16),
        pltpu.VMEM((16, cols, W), BF16),
        pltpu.VMEM((ZS, 3, cols, W), BF16),
        pltpu.VMEM((ZS, 3, cols, W), BF16),
        pltpu.VMEM((2, ZS, cols // 2, W), BF16),
        pltpu.VMEM((2, ZS, cols // 2, W), BF16),
        pltpu.VMEM((2, cols, W), F32),
        pltpu.SMEM((2, 2, OWNERS), jnp.int32),
        dma((6,)),
        dma((LEVELS + 6,)),
        dma((LEVELS, 2)),
        dma((2, 4)),
        dma((2, 2, 2)),
        dma((2, 2, 2)),
        dma((2,)),
        dma((2, 2, 3, 3)),
        dma((2, ZS, 3)),
        dma((2, 3, ZS)),
    ]
    smem = pl.BlockSpec(memory_space=pltpu.SMEM)
    anywhere = pl.BlockSpec(memory_space=pl.ANY)
    return pl.pallas_call(
        kernel,
        out_shape=pltpu.VMEM(noise_draws.shape, BF16),
        in_specs=[smem, smem, smem, anywhere, anywhere, anywhere],
        out_specs=pl.BlockSpec(memory_space=pltpu.VMEM),
        scratch_shapes=scratch,
        compiler_params=pltpu.CompilerParams(
            collective_id=0, has_side_effects=True, vmem_limit_bytes=60 * 1024 * 1024
        ),
    )(ancestor_pick, coupling_lists, live_counts, noise_draws, inverse_diagonal, coupling_blocks)


def solution(mesh):
    placed = (
        P(None, "leaf", None, "draw"),
        P(None, "leaf", "draw", None),
        P(None, "leaf", "draw", None, None),
        P(),
        P(None, "leaf", None),
        P(None, "leaf"),
    )
    return jax.shard_map(
        on_device,
        mesh=mesh,
        in_specs=placed,
        out_specs=P(None, "leaf", None, "draw"),
        check_vma=False,
    )
```

time: 127 us -> 123 us (0.969); the launches traced: 125 us -> 123 us
  Pallas kernels: 123 us -> 121 us
    pallas_call x1, Pallas kernels: 123 us -> 121 us  [on_device(): pl.pallas_call(kernel, out_shape=pltpu.VMEM(noise_draws.shape, BF16), in_...]
where the time goes in v3:
time: 123 us
  Pallas kernels  121 us (98%)
    pallas_call x1, Pallas kernels, on_device(): pl.pallas_call(kernel, out_shape=pltpu.VMEM(noise_draws.shape, BF16), in_...  121 us

profile of v3, /device:TPU:1, one launch (start us, length us, event | category | flops | bytes accessed | tf_op | source)
XLA Modules:
  0.0 122.6 jit_solution(14085164886177314621)
XLA Ops:
  0.0 121.4 %shard_map.64 = bf16[3,2,256,512]{3,2,1,0:T(8,128)(2,1)S(1)} custom-call(s32[2,16,16]{2,1,0:T(8,128)} %pick.1, s32[2,2,16]{2,1,0:T(2,128)} %lists.1, s32[2,2]{1,0:T(2,128)} %counts.1, bf16[3,2,256,512]{3,2,1,0:T(8,128)(2,1)} %noise.1, bf16[3,2,16,256]{3,2,1,0:T(8,128)(2,1)} %inverse.1, bf16[2,2,1,256,256]{4,3,2,1,0:T(8,128)(2,1)} %blocks.1), custom_call_target="tpu_custom_call" | custom-call | tf_op jit(solution)/shard_map/pallas_call | solution.py:477
  121.4 1.1 copy.8

commit v4 on v3

--- a/solution.py
+++ b/solution.py
@@ -43,6 +43,7 @@
         return zh_ * (XS * CORES) + x_ * CORES + c_
 
     inside = jnp.logical_and(zl > 0, zl < ZS - 1)
+    outside = jnp.logical_not(inside)
     def move(src, dst, s_sem, r_sem, device):
         return pltpu.make_async_remote_copy(
             src_ref=src, dst_ref=dst, send_sem=s_sem, recv_sem=r_sem, device_id=device, device_id_type=MESH
@@ -103,9 +104,12 @@
     inverse_own = [pltpu.make_async_copy(inv_src[g], inv_dst[g](draw), loc.at[1 + g]) for g in range(LEVELS)]
     blocks_own = [pltpu.make_async_copy(blocks.at[l, :, 0], bf[l].at[draw], loc.at[4 + l]) for l in (0, 1)]
 
-    def blocks_z(l):
-        put(blocks.at[l, 0, 0], zrel.at[l, 0], sent.at[LEVELS + l], zr.at[l, 0], z_up2)
-        put(blocks.at[l, 1, 0], zrel.at[l, 1], sent.at[LEVELS + l], zr.at[l, 1], z_down2)
+    def blocks_z(l, cond=None):
+        plan = [
+            (blocks.at[l, 0, 0], zrel.at[l, 0], sent.at[LEVELS + l], zr.at[l, 0], z_up2),
+            (blocks.at[l, 1, 0], zrel.at[l, 1], sent.at[LEVELS + l], zr.at[l, 1], z_down2),
+        ]
+        run(plan, cond)
 
     def blocks_relay(l, cond=None):
         k_up = slot(lax.div(up(z, -2, RING), ZS), x, c)
@@ -171,14 +175,16 @@
         send[a][s, 2, rows(part)] = wanted(-1)
         table[a][src, rows(part)] = wanted(0)
 
-    def send_y(a, s, i, part):
+    def send_far(a, s, i, part):
+        way = part[2]
+        return [(
+            send[a].at[s, 0, rows(part)], relay[a].at[way, s, relay_rows(part)], sent.at[LEVELS + 2 + a],
+            yrel.at[a, i, s], (north, south)[way],
+        )]
+
+    def send_near(a, s, part):
         dst = table[a].at[y * ZS + s, rows(part)]
-        way = part[2]
         return [
-            (
-                send[a].at[s, 0, rows(part)], relay[a].at[way, s, relay_rows(part)], sent.at[LEVELS + 2 + a],
-                yrel.at[a, i, s], (north, south)[way],
-            ),
             (send[a].at[s, 1, rows(part)], dst, sent.at[LEVELS + 2 + a], yr.at[a, s, 0], north),
             (send[a].at[s, 2, rows(part)], dst, sent.at[LEVELS + 2 + a], yr.at[a, s, 1], south),
         ]
@@ -197,7 +203,7 @@
         choose(a, zl, part, lambda n: own[a][n, rows(part)])
         put(own[a].at[:, rows(part)], below[a][0][h], sent.at[LEVELS + 4 + a], lr.at[a, 0, 0, h], z_up, cond=zl < ZS - 1)
         put(own[a].at[:, rows(part)], above[a][0][h], sent.at[LEVELS + 4 + a], lr.at[a, 1, 0, h], z_down, cond=zl > 0)
-        run(send_y(a, zl, h, part))
+        run(send_far(a, zl, h, part) + send_near(a, zl, part))
 
     def follow(a, r, i):
         part = parts(r)[i]
@@ -217,17 +223,23 @@
                 run(sends, jnp.logical_and(here, more))
         for line, way, device, here, more, s in lines:
             pl.when(here)(lambda line=line, s=s: choose(a, s, part, lambda n: line[a][r - 1][i][n]))
-            run(send_y(a, s, i, part), here)
-
-    def by_round(r, body):
+            run(send_far(a, s, i, part), here)
+        ready = {(ZS - 1, 1): [], (ZS - 1, 2): parts(r)[1:]}.get((r, i), [part])
+        for line, way, device, here, more, s in lines:
+            run([step for each in ready for step in send_near(a, s, each)], here)
+
+    def both(cond, only):
+        return cond if only is None else only if cond is None else jnp.logical_and(cond, only)
+
+    def by_round(r, body, only):
         if r == 0:
-            body(zl, None)
+            body(zl, only)
         else:
-            body(zl - r, zl >= r)
-            body(zl + r, zl <= ZS - 1 - r)
-
-    def hand_on(a, r, i):
-        by_round(r, lambda s, cond: run(pass_y(a, s, i, parts(r)[i]), cond))
+            body(zl - r, both(zl >= r, only))
+            body(zl + r, both(zl <= ZS - 1 - r, only))
+
+    def hand_on(a, r, i, only=None):
+        by_round(r, lambda s, cond: run(pass_y(a, s, i, parts(r)[i]), cond), only)
 
     def add_source(a, src):
         if a == 0:
@@ -249,7 +261,7 @@
         else:
             pl.when(cond)(body)
 
-    def use_near(a, r):
+    def use_near(a, r, only=None):
         def body(s, cond):
             def inner():
                 add_source(a, y * ZS + s)
@@ -260,9 +272,9 @@
 
             guarded(cond, inner)
 
-        by_round(r, body)
-
-    def use_far(a, r):
+        by_round(r, body, only)
+
+    def use_far(a, r, only=None):
         def body(s, cond):
             def inner():
                 src = up(y, 2, YS) * ZS + s
@@ -271,7 +283,7 @@
 
             guarded(cond, inner)
 
-        by_round(r, body)
+        by_round(r, body, only)
 
     def find_places():
         @pl.loop(0, OWNERS)
@@ -323,7 +335,7 @@
         left(LEVELS + a, table[a])
         left(LEVELS + 2 + a, table[a])
         pl.when(inside)(lambda: left(LEVELS + 4 + a, table[a].at[pl.ds(0, 10)]))
-        pl.when(jnp.logical_not(inside))(lambda: left(LEVELS + 4 + a, table[a].at[pl.ds(0, 2)]))
+        pl.when(outside)(lambda: left(LEVELS + 4 + a, table[a].at[pl.ds(0, 2)]))
 
     for copy in inverse_own + blocks_own:
         copy.start()
@@ -344,41 +356,45 @@
     blocks_out(0, 0)
     find_places()
     inverse_first(1)
+    hand_on(0, 0, 0)
+    hand_on(0, 0, 1)
     follow(0, 1, 0)
-    hand_on(0, 0, 0)
     blocks_x(0, 0)
     blocks_far(0)
     follow(0, 1, 1)
-    hand_on(0, 0, 1)
+    hand_on(0, 1, 0, outside)
     clear()
     flip(1)
     blocks_x2(0, 0)
     follow(0, 2, 0)
+    hand_on(0, 1, 0, inside)
     blocks_x(0, 1)
+    hand_on(0, 1, 1, outside)
     inverse_next(1)
     follow(0, 2, 1)
-    hand_on(0, 1, 0)
+    hand_on(0, 1, 1, inside)
     blocks_x2(0, 1)
     blocks_out(1, 0)
-    hand_on(0, 1, 1)
+    blocks_z(1, outside)
+    hand_on(0, 2, 0, outside)
     blocks_wait(0)
-    use_near(0, 0)
+    use_near(0, 0, outside)
+    hand_on(0, 2, 0, inside)
     follow(0, 3, 0)
-    hand_on(0, 2, 0)
+    hand_on(0, 2, 1)
+    use_near(0, 0, inside)
     use_far(0, 0)
     follow(0, 3, 1)
     use_near(0, 1)
-    hand_on(0, 2, 1)
     follow(0, 3, 2)
-    blocks_z(1)
+    blocks_z(1, inside)
+    hand_on(0, 3, 0)
     blocks_x(1, 0)
-    hand_on(0, 3, 0)
+    use_far(0, 1)
     blocks_relay(1, inside)
-    use_far(0, 1)
+    hand_on(0, 3, 1)
     use_near(0, 2)
-    hand_on(0, 3, 1)
     hand_on(0, 3, 2)
-    blocks_relay(1, jnp.logical_not(inside))
     use_far(0, 2)
     inverse_own[1].wait()
     inverse_wait(1)
@@ -390,39 +406,42 @@
         for n in (0, 1):
             own1[n, rows(parts(0)[h])] = solve(1, n, parts(0)[h])
         first(1, h)
+    blocks_relay(1, outside)
     clear()
     show(0, own0)
     flip(2)
+    hand_on(1, 0, 0)
+    hand_on(1, 0, 1)
     follow(1, 1, 0)
-    hand_on(1, 0, 0)
     show(1, own1)
     follow(1, 1, 1)
-    hand_on(1, 0, 1)
+    hand_on(1, 1, 0, outside)
     follow(1, 2, 0)
+    hand_on(1, 1, 0, inside)
+    hand_on(1, 1, 1, outside)
     blocks_far(1)
     inverse_across(2)
     inverse_first(2)
     follow(1, 2, 1)
-    hand_on(1, 1, 0)
+    hand_on(1, 1, 1, inside)
     blocks_x(1, 1)
-    hand_on(1, 1, 1)
+    hand_on(1, 2, 0)
     follow(1, 3, 0)
-    hand_on(1, 2, 0)
+    hand_on(1, 2, 1)
     blocks_x2(1, 1)
     blocks_wait(1)
-    add_lower()
     settle(0)
     follow(1, 3, 1)
-    hand_on(1, 2, 1)
     use_near(1, 0)
+    follow(1, 3, 2)
     use_far(1, 0)
-    follow(1, 3, 2)
+    hand_on(1, 3, 0)
+    add_lower()
+    inverse_next(2)
     use_near(1, 1)
-    hand_on(1, 3, 0)
-    inverse_next(2)
     use_far(1, 1)
+    hand_on(1, 3, 1)
     use_near(1, 2)
-    hand_on(1, 3, 1)
     hand_on(1, 3, 2)
     use_far(1, 2)
     use_near(1, 3)

time: 123 us -> 119 us (0.967)
  Pallas kernels: 121 us -> 118 us
    pallas_call x1, Pallas kernels: 121 us -> 118 us  [on_device(): pl.pallas_call(kernel, out_shape=pltpu.VMEM(noise_draws.shape, BF16), in_...]
where the time goes in v4:
time: 119 us
  Pallas kernels  118 us (99%)
    pallas_call x1, Pallas kernels, on_device(): pl.pallas_call(kernel, out_shape=pltpu.VMEM(noise_draws.shape, BF16), in_...  118 us

profile of v4, /device:TPU:1, one launch (start us, length us, event | category | flops | bytes accessed | tf_op | source)
XLA Modules:
  0.0 118.8 jit_solution(6928439622952328023)
XLA Ops:
  0.0 117.7 %shard_map.64 = bf16[3,2,256,512]{3,2,1,0:T(8,128)(2,1)S(1)} custom-call(s32[2,16,16]{2,1,0:T(8,128)} %pick.1, s32[2,2,16]{2,1,0:T(2,128)} %lists.1, s32[2,2]{1,0:T(2,128)} %counts.1, bf16[3,2,256,512]{3,2,1,0:T(8,128)(2,1)} %noise.1, bf16[3,2,16,256]{3,2,1,0:T(8,128)(2,1)} %inverse.1, bf16[2,2,1,256,256]{4,3,2,1,0:T(8,128)(2,1)} %blocks.1), custom_call_target="tpu_custom_call" | custom-call | tf_op jit(solution)/shard_map/pallas_call | solution.py:496
  117.7 1.1 copy.8

commit v5 on v4

--- a/solution.py
+++ b/solution.py
@@ -72,7 +72,7 @@
             pl.when(cond)(body)
 
     barrier = pltpu.get_barrier_semaphore()
-    peers = [(leaf, zh * (XS * CORES) + lax.rem(q + j, XS * CORES)) for j in range(1, XS * CORES)]
+    peers = [(leaf, zh * (XS * CORES) + lax.rem(q + j, XS * CORES)) for j in (4, 3, 5, 2, 6, 1, 7)]
     greeted = peers + [partner, z_up, z_down, z_up2, z_down2, north, south]
     noise_in = pltpu.make_async_copy(noise, noise_v, loc.at[0])
     noise_in.start()
@@ -104,22 +104,27 @@
     inverse_own = [pltpu.make_async_copy(inv_src[g], inv_dst[g](draw), loc.at[1 + g]) for g in range(LEVELS)]
     blocks_own = [pltpu.make_async_copy(blocks.at[l, :, 0], bf[l].at[draw], loc.at[4 + l]) for l in (0, 1)]
 
+    def halves(ref):
+        return [ref.at[pl.ds(p * (W // 2), W // 2)] for p in (0, 1)]
+
+    ways = ((0, z_up2, -2), (1, z_down2, 2))
+
     def blocks_z(l, cond=None):
-        plan = [
-            (blocks.at[l, 0, 0], zrel.at[l, 0], sent.at[LEVELS + l], zr.at[l, 0], z_up2),
-            (blocks.at[l, 1, 0], zrel.at[l, 1], sent.at[LEVELS + l], zr.at[l, 1], z_down2),
-        ]
+        plan = []
+        for p in (0, 1):
+            for n, device, _ in ways:
+                src, dst = halves(blocks.at[l, n, 0])[p], halves(zrel.at[l, n])[p]
+                plan.append((src, dst, sent.at[LEVELS + l], zr.at[l, 0, n, p], device))
         run(plan, cond)
 
     def blocks_relay(l, cond=None):
-        k_up = slot(lax.div(up(z, -2, RING), ZS), x, c)
-        k_down = slot(lax.div(up(z, 2, RING), ZS), x, c)
-        plan = [
-            (zrel.at[l, 0], zr.at[l, 0]),
-            (zrel.at[l, 0], bf[l].at[k_up, 0], sent.at[LEVELS + l], zr.at[l, 2], z_up2),
-            (zrel.at[l, 1], zr.at[l, 1]),
-            (zrel.at[l, 1], bf[l].at[k_down, 1], sent.at[LEVELS + l], zr.at[l, 3], z_down2),
-        ]
+        plan = []
+        for p in (0, 1):
+            for n, device, back in ways:
+                k = slot(lax.div(up(z, back, RING), ZS), x, c)
+                held, dst = halves(zrel.at[l, n])[p], halves(bf[l].at[k, n])[p]
+                plan.append((held, zr.at[l, 0, n, p]))
+                plan.append((held, dst, sent.at[LEVELS + l], zr.at[l, 1, n, p], device))
         run(plan, cond)
 
     def blocks_out(l, u):
@@ -130,8 +135,9 @@
         put(src, bf[l].at[k], sent.at[LEVELS + l], cr.at[l], other)
 
     def blocks_far(l):
-        got(bf[l].at[far, 0], zr.at[l, 2])
-        got(bf[l].at[far, 1], zr.at[l, 3])
+        for n in (0, 1):
+            for p in (0, 1):
+                got(halves(bf[l].at[far, n])[p], zr.at[l, 1, n, p])
         blocks_out(l, 1)
 
     def blocks_x(l, u):
@@ -388,6 +394,7 @@
     use_near(0, 1)
     follow(0, 3, 2)
     blocks_z(1, inside)
+    inverse_across(2)
     hand_on(0, 3, 0)
     blocks_x(1, 0)
     use_far(0, 1)
@@ -420,7 +427,6 @@
     hand_on(1, 1, 0, inside)
     hand_on(1, 1, 1, outside)
     blocks_far(1)
-    inverse_across(2)
     inverse_first(2)
     follow(1, 2, 1)
     hand_on(1, 1, 1, inside)
@@ -483,7 +489,7 @@
         dma((6,)),
         dma((LEVELS + 6,)),
         dma((LEVELS, 2)),
-        dma((2, 4)),
+        dma((2, 2, 2, 2)),
         dma((2, 2, 2)),
         dma((2, 2, 2)),
         dma((2,)),

time: 119 us -> 118 us (level)
  no operation moved by 1% of the time
where the time goes in v5:
time: 118 us
  Pallas kernels  117 us (99%)
    pallas_call x1, Pallas kernels, on_device(): pl.pallas_call(kernel, out_shape=pltpu.VMEM(noise_draws.shape, BF16), in_...  117 us

profile of v5, /device:TPU:1, one launch (start us, length us, event | category | flops | bytes accessed | tf_op | source)
XLA Modules:
  0.0 118.3 jit_solution(12332829470242580781)
XLA Ops:
  0.0 117.2 %shard_map.64 = bf16[3,2,256,512]{3,2,1,0:T(8,128)(2,1)S(1)} custom-call(s32[2,16,16]{2,1,0:T(8,128)} %pick.1, s32[2,2,16]{2,1,0:T(2,128)} %lists.1, s32[2,2]{1,0:T(2,128)} %counts.1, bf16[3,2,256,512]{3,2,1,0:T(8,128)(2,1)} %noise.1, bf16[3,2,16,256]{3,2,1,0:T(8,128)(2,1)} %inverse.1, bf16[2,2,1,256,256]{4,3,2,1,0:T(8,128)(2,1)} %blocks.1), custom_call_target="tpu_custom_call" | custom-call | tf_op jit(solution)/shard_map/pallas_call | solution.py:502
  117.2 1.1 copy.8
